TPU v7x, 32 devices: a whole 2x2x4 slice. The times are simulated.
32 devices in a mesh: span: 8 (over z, x), tensor: 4 (over y, core).
Axes of the slice: x: 2, y: 2, z: 4, core: 2. Of those that a mesh axis runs over, the one named last changes fastest.
Arguments:
- latents: bfloat16 [1024, 5120], P(('span', 'tensor')), may hold values from -6 to 6
- modulation: float32 [4, 3, 5120], replicated, may hold values from -3 to 3
- w_query: bfloat16 [5120, 4096], P(None, 'tensor'), may hold values from -0.078125 to 0.078125
- w_key: bfloat16 [5120, 4096], P(None, 'tensor'), may hold values from -0.078125 to 0.078125
- w_value: bfloat16 [5120, 4096], P(None, 'tensor'), may hold values from -0.078125 to 0.078125
- w_out: bfloat16 [4096, 5120], P('tensor'), may hold values from -0.5 to 0.5
- cache_k: bfloat16 [2048, 4096], P('span', 'tensor'), may hold values from -800 to 800
- cache_v: bfloat16 [2048, 4096], P('span', 'tensor'), may hold values from -6 to 6
- level_index: int32 [8], P('span'), may hold values from 0 to 3
- rotation: int32 [8], replicated, may hold values from 0 to 7, each once
- cached_tokens: int32 [1], replicated, may hold values from 128 to 2048
Outputs:
- branch: bfloat16 [1024, 5120], P(('span', 'tensor'))
All inputs are finite; a program needn't handle non-finite values.
Results may differ from a plain program's by a relative error of at most 0.019.
Values may be sent and summed in bfloat16 or wider, within the bound.
No kernel may reach another device: no remote copies, remote signals or barrier semaphores. Data moves between devices by JAX's collectives and lax.ppermute only.
A program may use at most 128 MiB of HBM per device.

v0:
```python
import jax
import jax.numpy as jnp
from jax import lax
from jax.sharding import PartitionSpec as P

HD = 128
EPSILON = 1e-06


def block_update(running, q_heads, key_block, value_block, key_valid):
    run_max, run_sum, run_acc = running
    head_count = q_heads.shape[1]
    head_size = q_heads.shape[2]
    key_heads = key_block.reshape(key_block.shape[0], head_count, head_size)
    value_heads = value_block.reshape(value_block.shape[0], head_count, head_size)
    scores = jnp.einsum(
        "qhd,khd->hqk", q_heads, key_heads, preferred_element_type=jnp.float32
    ) * head_size ** (-0.5)
    scores = jnp.where(key_valid[None, None, :], scores, -1e30)
    new_max = jnp.maximum(run_max, jnp.max(scores, axis=-1))
    weights = jnp.where(key_valid[None, None, :], jnp.exp(scores - new_max[..., None]), 0.0)
    rescale = jnp.exp(run_max - new_max)
    run_sum = run_sum * rescale + jnp.sum(weights, axis=-1)
    run_acc = run_acc * rescale[..., None] + jnp.einsum(
        "hqk,khd->hqd",
        weights.astype(jnp.bfloat16),
        value_heads,
        preferred_element_type=jnp.float32,
    )
    return (new_max, run_sum, run_acc)


def attend(running, q_heads, key_rows, value_rows, key_valid):
    running = block_update(running, q_heads, key_rows, value_rows, key_valid)
    return running


def body(
    latents,
    modulation,
    w_query,
    w_key,
    w_value,
    w_out,
    cache_k,
    cache_v,
    level_index,
    rotation,
    cached_tokens,
):
    groups = lax.axis_size("span")
    own_index = lax.axis_index("span")
    chooser = (jnp.arange(modulation.shape[0], dtype=jnp.int32) == level_index[0]).astype(
        jnp.float32
    )
    mod_rows = jnp.sum(chooser[:, None, None] * modulation, axis=0)
    shift_row, scale_row, gate_row = (mod_rows[0], mod_rows[1], mod_rows[2])
    row_data = latents.astype(jnp.float32)
    row_mean = jnp.mean(row_data, axis=-1, keepdims=True)
    centred = row_data - row_mean
    row_var = jnp.mean(centred * centred, axis=-1, keepdims=True)
    normed = centred * lax.rsqrt(row_var + EPSILON)
    modulated = (normed * (1.0 + scale_row) + shift_row).astype(jnp.bfloat16)
    shard_piece = lax.all_gather(modulated, "tensor", axis=0, tiled=True)
    projected = [
        jnp.dot(shard_piece, weight, preferred_element_type=jnp.float32).astype(jnp.bfloat16)
        for weight in (w_query, w_key, w_value)
    ]
    joined = jnp.concatenate(projected, axis=1)
    inner_width = w_query.shape[1]
    own_query = joined[:, :inner_width]
    own_key = joined[:, inner_width : 2 * inner_width]
    own_value = joined[:, 2 * inner_width :]
    head_count = inner_width // HD
    span_rows = own_query.shape[0]
    q_heads = own_query.reshape(span_rows, head_count, HD)
    group_ids = jnp.arange(groups, dtype=jnp.int32)
    order_own = jnp.sum(jnp.where(group_ids == own_index, rotation, 0))
    live_keys = cached_tokens[0]
    initial = (
        jnp.full((head_count, span_rows), -1e30, jnp.float32),
        jnp.zeros((head_count, span_rows), jnp.float32),
        jnp.zeros((head_count, span_rows, HD), jnp.float32),
    )
    all_queries = lax.all_gather(own_query, "span", axis=0, tiled=True)
    cache_rows = cache_k.shape[0]
    local_valid = own_index * cache_rows + jnp.arange(cache_rows, dtype=jnp.int32) < live_keys

    def group_partial(group_queries):
        return attend(initial, group_queries, cache_k, cache_v, local_valid)

    partials = lax.map(group_partial, all_queries.reshape(groups, span_rows, head_count, HD))
    source_max, source_sum, source_acc = lax.all_to_all(
        partials, "span", split_axis=0, concat_axis=0, tiled=True
    )
    best_max = jnp.max(source_max, axis=0)
    rescale = jnp.exp(source_max - best_max)
    running = (
        best_max,
        jnp.sum(source_sum * rescale, axis=0),
        jnp.sum(source_acc * rescale[..., None], axis=0),
    )
    key_rows = lax.all_gather(own_key, "span", axis=0, tiled=True)
    value_rows = lax.all_gather(own_value, "span", axis=0, tiled=True)
    key_index = jnp.arange(key_rows.shape[0], dtype=jnp.int32)
    key_group = key_index // span_rows
    key_order = jnp.sum(
        jnp.where(key_group[:, None] == group_ids[None, :], rotation[None, :], 0), axis=1
    )
    key_valid = key_order <= order_own
    run_max, run_sum, run_acc = attend(running, q_heads, key_rows, value_rows, key_valid)
    attended = (
        (run_acc / run_sum[..., None])
        .transpose(1, 0, 2)
        .reshape(span_rows, inner_width)
        .astype(jnp.bfloat16)
    )
    projection = lax.psum_scatter(
        jnp.dot(attended, w_out, preferred_element_type=jnp.float32).astype(jnp.bfloat16),
        "tensor",
        scatter_dimension=0,
        tiled=True,
    ).astype(jnp.float32)
    return (gate_row[None, :] * projection).astype(jnp.bfloat16)


def solution(mesh):
    placed = (
        P(("span", "tensor"), None),
        P(),
        P(None, "tensor"),
        P(None, "tensor"),
        P(None, "tensor"),
        P("tensor", None),
        P("span", "tensor"),
        P("span", "tensor"),
        P("span"),
        P(),
        P(),
    )
    return jax.shard_map(
        body, mesh=mesh, in_specs=placed, out_specs=P(("span", "tensor"), None), check_vma=False
    )
```

profile of v0, /device:TPU:0, one launch (start us, length us, event | category | flops | bytes accessed | tf_op | source)
XLA Modules:
  0.0 317.0 jit_solution(9142673391689891589)
XLA Ops:
  7.2 1.2 multiply_reduce_fusion.1
  8.4 1.1 convert_reduce_fusion
  9.6 1.2 fusion.46
  10.8 1.9 fusion.49
  12.8 21.0 %all-gather.5.cloned.1.call-done = bf16[128,5120]{1,0:T(8,128)(2,1)} async-done(((bf16[32,5120]{1,0:T(8,128)(2,1)}), bf16[128,5120]{1,0:T(8,128)(2,1)}) %all-gather.5.cloned.1.call-update) | async-done | bytes 1310736 | tf_op jit(solution)/shard_map/all_gather | solution.py:64
  33.8 6.7 %convolution_convert_fusion.3 = bf16[128,1024]{1,0:T(8,128)(2,1)} fusion(bf16[128,5120]{1,0:T(8,128)(2,1)} %all-gather.5.cloned.1.call-done, bf16[5120,1024]{1,0:T(8,128)(2,1)} %param.15), kind=kOutput, calls=%fused_computation.48 | convolution fusion | flops 1342308352 | bytes 12058624 | tf_op jit(solution)/shard_map/dot_general | solution.py:66
  40.6 6.2 %convolution_convert_fusion.1 = bf16[128,1024]{1,0:T(8,128)(2,1)} fusion(bf16[128,5120]{1,0:T(8,128)(2,1)S(1)} %copy-done, bf16[5120,1024]{1,0:T(8,128)(2,1)} %param.17), kind=kOutput, calls=%fused_computation.46 | convolution fusion | flops 1342308352 | bytes 12058624 | tf_op jit(solution)/shard_map/dot_general | solution.py:66
  46.9 42.9 %all-gather.7.cloned.1.call-done = bf16[1024,1024]{1,0:T(8,128)(2,1)} async-done(((bf16[128,1024]{1,0:T(8,128)(2,1)}), bf16[1024,1024]{1,0:T(8,128)(2,1)}) %all-gather.7.cloned.1.call-update) | async-done | bytes 2097168 | tf_op jit(solution)/shard_map/all_gather | solution.py:85
  89.8 2.2 copy.38
  92.0 38.5 %while.15 = (s32[]{:T(128)}, f32[8,8,128]{2,1,0:T(8,128)S(1)}, f32[8,8,128]{2,1,0:T(8,128)S(1)}, f32[8,8,128,128]{3,2,1,0:T(8,128)}, bf16[8,128,8,128]{3,2,1,0:T...) while((s32[]{:T(128)}, f32[8,8,128]{2,1,0:T(8,128)S(1)}, ...), condition=%wide.region_6.7_spmd.clone, body=%wide.region_3.6_spmd.clone.sunk | while | flops 136713728 | bytes 5555829 | solution.py:92
  92.0 0.7 add_compare_fusion.2
  92.7 1.4 fusion.88
  94.2 2.2 fusion.91
  96.8 0.7 add_compare_fusion.2
  97.5 1.5 fusion.88
  99.0 2.2 fusion.91
  101.7 0.7 add_compare_fusion.2
  102.3 1.4 fusion.88
  103.8 2.2 fusion.91
  106.4 0.7 add_compare_fusion.2
  107.1 1.4 fusion.88
  108.6 2.2 fusion.91
  111.2 0.7 add_compare_fusion.2
  111.9 1.4 fusion.88
  113.4 2.2 fusion.91
  116.0 0.7 add_compare_fusion.2
  116.7 1.5 fusion.88
  118.3 2.2 fusion.91
  121.0 0.7 add_compare_fusion.2
  121.6 1.4 fusion.88
  123.1 2.2 fusion.91
  125.7 0.7 add_compare_fusion.2
  126.4 1.4 fusion.88
  127.8 2.2 fusion.91
  130.5 9.8 %all_to_all.15 = f32[8,8,128]{2,1,0:T(8,128)S(1)} all-to-all(f32[8,8,128]{2,1,0:T(8,128)S(1)} %get-tuple-element.50), channel_id=1, replica_groups=mesh['span'=8,'tensor'=4] {'span'}, dimensions={0} | all-to-all | bytes 65536 | tf_op jit(solution)/shard_map/all_to_all | solution.py:93
  140.3 9.0 %all_to_all.16 = f32[8,8,128]{2,1,0:T(8,128)S(1)} all-to-all(f32[8,8,128]{2,1,0:T(8,128)S(1)} %get-tuple-element.51), channel_id=1, replica_groups=mesh['span'=8,'tensor'=4] {'span'}, dimensions={0} | all-to-all | bytes 65536 | tf_op jit(solution)/shard_map/all_to_all | solution.py:93
  149.4 4.5 %all-to-all-start = ((f32[8,8,128,128]{3,2,1,0:T(8,128)}), f32[8,8,128,128]{3,2,1,0:T(8,128)}, u32[]{:S(2)}, u32[]{:S(2)}) async-start(f32[8,8,128,128]{3,2,1,0:T(8,128)} %get-tuple-element.49), calls=%async_computation | async-start | bytes 8388608 | tf_op jit(solution)/shard_map/all_to_all | solution.py:93
  154.0 6.2 %convolution_convert_fusion.2 = bf16[128,1024]{1,0:T(8,128)(2,1)} fusion(bf16[128,5120]{1,0:T(8,128)(2,1)S(1)} %copy-done, bf16[5120,1024]{1,0:T(8,128)(2,1)} %param.16), kind=kOutput, calls=%fused_computation.47 | convolution fusion | flops 1342308352 | bytes 12058624 | tf_op jit(solution)/shard_map/dot_general | solution.py:66
  161.7 2.9 copy.32
  164.6 92.7 %all-gather.9.cloned.1.call-done = bf16[1024,1024]{1,0:T(8,128)(2,1)} async-done(((bf16[128,1024]{1,0:T(8,128)(2,1)}), bf16[1024,1024]{1,0:T(8,128)(2,1)}) %all-gather.9.cloned.1.call-update) | async-done | bytes 2097168 | tf_op jit(solution)/shard_map/all_gather | solution.py:103
  257.3 4.5 %fusion.19 = (f32[8,128]{1,0:T(8,128)S(1)}, f32[8,128,1024]{2,1,0:T(8,128)}) fusion(pred[1024]{0:T(1024)(128)(4,1)S(1)} %broadcast_compare_fusion, bf16[1024,1024]{1,0:T(8,128)(2,1)} %all-gather.9.cloned.1.call-done, bf16[128,1024]{1,0:T(8,128)(2,1)S(1)} %copy-done.1), kind=kOutput, calls=%fused_computation.32 | convolution fusion | flops 271580160 | bytes 6558720 | tf_op jit(solution)/shard_map/qhd,khd->hqk/dot_general | solution.py:16
  261.8 3.3 %fusion.20 = f32[8,128]{1,0:T(8,128)S(1)} fusion(f32[8,128,1024]{2,1,0:T(8,128)} %get-tuple-element.133, f32[8,128]{1,0:T(8,128)S(1)} %max.18, pred[1024]{0:T(1024)(128)(4,1)S(1)} %broadcast_compare_fusion), kind=kLoop, calls=%fused_computation.33 | loop fusion | flops 5241856 | bytes 4203520 | tf_op jit(solution)/shard_map/reduce_sum | solution.py:23
  265.1 4.8 %all-to-all-done = f32[8,8,128,128]{3,2,1,0:T(8,128)} async-done(((f32[8,8,128,128]{3,2,1,0:T(8,128)}), f32[8,8,128,128]{3,2,1,0:T(8,128)}, u32[]{:S(2)}, u32[]{:S(2)}) %all-to-all-start) | async-done | bytes 4194336 | tf_op jit(solution)/shard_map/all_to_all | solution.py:93
  269.9 2.9 multiply_reduce_fusion
  273.0 3.6 %fusion.41 = bf16[128,8,128]{0,2,1:T(8,128)(2,1)S(1)} fusion(bf16[1024,8,128]{0,2,1:T(8,128)(2,1)S(1)} %bitcast.117, f32[8,128,1024]{2,1,0:T(8,128)} %get-tuple-element.133, f32[8,128]{1,0:T(8,128)S(1)} %max.18, pred[1024]{0:T(1024)(128)(4,1)S(1)} %broadcast_compare_fusion, f32[8,128,128]{1,2,0:T(8,128)S(1)} %copy.28, f32[128,8]{0,1:T(8,128)S(1)} %get-tuple-element.119, ...), kind=kOutput, calls=%fused_computation.50 | convolution fusion | flops 274202624 | bytes 7091200 | tf_op jit(solution)/shard_map/hqk,khd->hqd/dot_general | solution.py:24
  276.6 6.6 %convolution_convert_fusion = bf16[128,5120]{1,0:T(8,128)(2,1)} fusion(bf16[128,1024]{0,1:T(8,128)(2,1)S(1)} %bitcast.119, bf16[1024,5120]{1,0:T(8,128)(2,1)} %param.18), kind=kOutput, calls=%fused_computation.28 | convolution fusion | flops 1342832640 | bytes 12058624 | tf_op jit(solution)/shard_map/dot_general | solution.py:119
  283.2 25.5 %reduce-scatter.2.cloned.1.call-done = bf16[32,5120]{1,0:T(8,128)(2,1)} async-done(((bf16[128,5120]{1,0:T(8,128)(2,1)}), bf16[32,5120]{1,0:T(8,128)(2,1)}) %reduce-scatter.2.cloned.1.call-update) | async-done | bytes 327696 | tf_op jit(solution)/shard_map/reduce_scatter | solution.py:118
  308.7 1.8 multiply_convert_fusion
  (65 shorter events, 5.4 us)
Async XLA Ops:
  6.5 27.3 %all-gather.5.cloned.1.call-start = ((), (), s32[]{:S(2)}) async-start(), calls=%async_computation.4 | async-start | bytes 1638400 | tf_op jit(solution)/shard_map/all_gather | solution.py:64
  12.7 77.0 %all-gather.7.cloned.1.call-start = ((), (), s32[]{:S(2)}) async-start(), calls=%async_computation.5 | async-start | bytes 2359296 | tf_op jit(solution)/shard_map/all_gather | solution.py:85
  33.8 6.8 %copy-start = (bf16[128,5120]{1,0:T(8,128)(2,1)S(1)}, bf16[128,5120]{1,0:T(8,128)(2,1)}, u32[]{:S(2)}) copy-start(bf16[128,5120]{1,0:T(8,128)(2,1)} %all-gather.5.cloned.1.call-done) | copy-start | bytes 3932164
  40.5 121.2 %all-gather.11.cloned.1.call-start = ((), (), s32[]{:S(2)}) async-start(), calls=%async_computation.7 | async-start | bytes 2359296 | tf_op jit(solution)/shard_map/all_gather | solution.py:104
  149.4 120.5 %all-to-all-start = ((f32[8,8,128,128]{3,2,1,0:T(8,128)}), f32[8,8,128,128]{3,2,1,0:T(8,128)}, u32[]{:S(2)}, u32[]{:S(2)}) async-start(f32[8,8,128,128]{3,2,1,0:T(8,128)} %get-tuple-element.49), calls=%async_computation | async-start | bytes 8388608 | tf_op jit(solution)/shard_map/all_to_all | solution.py:93
  153.9 6.6 %copy-start.2 = (s32[8]{0:T(128)S(1)}, s32[8]{0:T(128)}, u32[]{:S(2)}) copy-start(s32[8]{0:T(128)} %param.22) | copy-start | bytes 100
  153.9 103.4 %all-gather.9.cloned.1.call-start = ((), (), s32[]{:S(2)}) async-start(), calls=%async_computation.6 | async-start | bytes 2359296 | tf_op jit(solution)/shard_map/all_gather | solution.py:103
  160.2 97.1 %copy-start.1 = (bf16[128,1024]{1,0:T(8,128)(2,1)S(1)}, bf16[128,1024]{1,0:T(8,128)(2,1)}, u32[]{:S(2)}) copy-start(bf16[128,1024]{1,0:T(8,128)(2,1)} %convolution_convert_fusion.3) | copy-start | bytes 786436
  160.2 148.5 %reduce-scatter.2.cloned.1.call-start = ((), (), s32[]{:S(2)}) async-start(), calls=%async_computation.8 | async-start | bytes 1638400 | tf_op jit(solution)/shard_map/reduce_scatter | solution.py:118
Sparse Core Ops, SparseCore 0:
  12.9 20.8 all-gather.4
  40.7 49.0 all-gather.6
  91.9 48.4 all-gather.10
  160.3 96.8 all-gather.8
  283.3 25.3 reduce-scatter.1
where the time goes:
time: 319 us; the launch traced here: 317 us
  waiting for transfers between devices  187 us (59%)
  matrix products  63.2 us (20%)
  other arithmetic  23.1 us (7%)
  blocking collectives  18.9 us (6%)
  between operations  14 us (4%)
  local copies, waits for them, and re-layouts  5.46 us (2%)
  starting transfers between devices  4.89 us (2%)
    all_gather x1, waiting for transfers between devices, body(): key_rows = lax.all_gather(own_key, 'span', axis=0, tiled=True)  92.7 us
    all_gather x1, waiting for transfers between devices, body(): all_queries = lax.all_gather(own_query, 'span', axis=0, tiled=True)  42.9 us
    reduce_scatter x1, waiting for transfers between devices, body(): lax.psum_scatter(jnp.dot(attended, w_out, preferred_element_type=jnp.floa...  25.5 us
    dot_general x9, matrix products, block_update(): jnp.einsum('hqk,khd->hqd', weights.astype(jnp.bfloat16), value_heads, pre...  21.4 us
    all_gather x1, waiting for transfers between devices, body(): shard_piece = lax.all_gather(modulated, 'tensor', axis=0, tiled=True)  21 us
    dot_general x3, matrix products, body(): jnp.dot(shard_piece, weight, preferred_element_type=jnp.float32)  19.1 us
    all_to_all x2, blocking collectives, body(): lax.all_to_all(partials, 'span', split_axis=0, concat_axis=0, tiled=True)  18.9 us
    dot_general x9, matrix products, block_update(): jnp.einsum('qhd,khd->hqk', q_heads, key_heads, preferred_element_type=jnp...  16.1 us
  transfers between devices with their start and end apart: 6, of which 5 were waited for; matrix products, arithmetic and copies ran while one was open for 20% of the time, Pallas kernels for 0%

commit v1 on v0

--- a/solution.py
+++ b/solution.py
@@ -100,7 +100,10 @@
         jnp.sum(source_sum * rescale, axis=0),
         jnp.sum(source_acc * rescale[..., None], axis=0),
     )
-    key_rows = lax.all_gather(own_key, "span", axis=0, tiled=True)
+    size = lax.axis_size("span")
+    tiles = jnp.stack([own_key for _ in range(size)])
+    tiles = lax.all_to_all(tiles, "span", split_axis=0, concat_axis=0)
+    key_rows = jnp.concatenate(tiles, axis=0)
     value_rows = lax.all_gather(own_value, "span", axis=0, tiled=True)
     key_index = jnp.arange(key_rows.shape[0], dtype=jnp.int32)
     key_group = key_index // span_rows

time: 319 us -> 360 us (1.13)
  waiting for transfers between devices: 187 us -> 211 us
  local copies, waits for them, and re-layouts: 5.46 us -> 19.3 us
  starting transfers between devices: 4.89 us -> 10.4 us
    all_gather x1, waiting for transfers between devices: 0.02 us -> 93.9 us  [body(): value_rows = lax.all_gather(own_value, 'span', axis=0, tiled=True)]
    all_gather x1 -> x0, waiting for transfers between devices: 92.7 us -> none  [body(): key_rows = lax.all_gather(own_key, 'span', axis=0, tiled=True)]
    all_gather x1, waiting for transfers between devices: 42.9 us -> 68.8 us  [body(): all_queries = lax.all_gather(own_query, 'span', axis=0, tiled=True)]
    dynamic_slice x8, local copies, waits for them, and re-layouts: 0.19 us -> 7.77 us  [body(): lax.map(group_partial, all_queries.reshape(groups, span_rows, head_count,...]
    all_to_all x0 -> x1, starting transfers between devices: none -> 5.51 us  [body(): tiles = lax.all_to_all(tiles, 'span', split_axis=0, concat_axis=0)]
  transfers between devices with their start and end apart: 6 -> 6, of which waited for: 5 -> 5; matrix products, arithmetic and copies ran while one was open for 20% -> 21% of each run, Pallas kernels for 0% -> 0%
where the time goes in v1:
time: 360 us; the launch traced here: 358 us
  waiting for transfers between devices  211 us (59%)
  matrix products  60.8 us (17%)
  other arithmetic  23.4 us (6%)
  local copies, waits for them, and re-layouts  19.3 us (5%)
  blocking collectives  18.1 us (5%)
  between operations  14 us (4%)
  starting transfers between devices  10.4 us (3%)
    all_gather x1, waiting for transfers between devices, body(): value_rows = lax.all_gather(own_value, 'span', axis=0, tiled=True)  93.9 us
    all_gather x1, waiting for transfers between devices, body(): all_queries = lax.all_gather(own_query, 'span', axis=0, tiled=True)  68.8 us
    reduce_scatter x1, waiting for transfers between devices, body(): lax.psum_scatter(jnp.dot(attended, w_out, preferred_element_type=jnp.floa...  25.2 us
    dot_general x9, matrix products, block_update(): jnp.einsum('hqk,khd->hqd', weights.astype(jnp.bfloat16), value_heads, pre...  21.4 us
    all_gather x1, waiting for transfers between devices, body(): shard_piece = lax.all_gather(modulated, 'tensor', axis=0, tiled=True)  21 us
    dot_general x3, matrix products, body(): jnp.dot(shard_piece, weight, preferred_element_type=jnp.float32)  18.4 us
    all_to_all x2, blocking collectives, body(): lax.all_to_all(partials, 'span', split_axis=0, concat_axis=0, tiled=True)  18.1 us
    dot_general x9, matrix products, block_update(): jnp.einsum('qhd,khd->hqk', q_heads, key_heads, preferred_element_type=jnp...  14.4 us
  transfers between devices with their start and end apart: 6, of which 5 were waited for; matrix products, arithmetic and copies ran while one was open for 21% of the time, Pallas kernels for 0%

profile of v1, /device:TPU:0, one launch (start us, length us, event | category | flops | bytes accessed | tf_op | source)
XLA Modules:
  0.0 357.7 jit_solution(4951630534873161786)
XLA Ops:
  7.2 1.2 multiply_reduce_fusion.1
  8.4 1.1 convert_reduce_fusion
  9.6 1.2 fusion.45
  10.8 1.9 fusion.48
  12.8 21.0 %all-gather.4.cloned.1.call-done = bf16[128,5120]{1,0:T(8,128)(2,1)} async-done(((bf16[32,5120]{1,0:T(8,128)(2,1)}), bf16[128,5120]{1,0:T(8,128)(2,1)}) %all-gather.4.cloned.1.call-update) | async-done | bytes 1310736 | tf_op jit(solution)/shard_map/all_gather | solution.py:64
  33.8 6.7 %convolution_convert_fusion.3 = bf16[128,1024]{1,0:T(8,128)(2,1)} fusion(bf16[128,5120]{1,0:T(8,128)(2,1)} %all-gather.4.cloned.1.call-done, bf16[5120,1024]{1,0:T(8,128)(2,1)} %param.15), kind=kOutput, calls=%fused_computation.47 | convolution fusion | flops 1342308352 | bytes 12058624 | tf_op jit(solution)/shard_map/dot_general | solution.py:66
  40.6 5.5 %convolution_convert_fusion.2 = bf16[128,1024]{1,0:T(8,128)(2,1)S(1)} fusion(bf16[128,5120]{1,0:T(8,128)(2,1)S(1)} %copy-done, bf16[5120,1024]{1,0:T(8,128)(2,1)} %param.16), kind=kOutput, calls=%fused_computation.46 | convolution fusion | flops 1342308352 | bytes 12058624 | tf_op jit(solution)/shard_map/dot_general | solution.py:66
  46.1 1.6 stack.2
  47.7 5.5 %all-to-all-start.2 = ((bf16[8,128,1024]{2,1,0:T(8,128)(2,1)}), bf16[8,128,1024]{2,1,0:T(8,128)(2,1)S(1)}, u32[]{:S(2)}, u32[]{:S(2)}) async-start(bf16[8,128,1024]{2,1,0:T(8,128)(2,1)} %stack.2), calls=%async_computation.2 | async-start | bytes 4194304 | tf_op jit(solution)/shard_map/all_to_all | solution.py:105
  53.2 68.8 %all-gather.6.cloned.1.call-done = bf16[1024,1024]{1,0:T(8,128)(2,1)} async-done(((bf16[128,1024]{1,0:T(8,128)(2,1)}), bf16[1024,1024]{1,0:T(8,128)(2,1)}) %all-gather.6.cloned.1.call-update) | async-done | bytes 2097168 | tf_op jit(solution)/shard_map/all_gather | solution.py:85
  122.0 3.5 copy.42
  125.6 45.9 %while.15 = (s32[]{:T(128)}, f32[8,8,128]{2,1,0:T(8,128)S(1)}, f32[8,8,128]{2,1,0:T(8,128)S(1)}, f32[8,8,128,128]{3,2,1,0:T(8,128)}, bf16[8,128,8,128]{3,2,1,0:T...) while((s32[]{:T(128)}, f32[8,8,128]{2,1,0:T(8,128)S(1)}, ...), condition=%wide.region_6.7_spmd.clone, body=%wide.region_3.6_spmd.clone.sunk | while | flops 136713728 | bytes 5555829 | solution.py:92
  127.2 1.4 fusion.86
  128.7 2.2 fusion.89
  131.3 1.0 constant_dynamic-slice_fusion.2
  132.9 1.4 fusion.86
  134.4 2.2 fusion.89
  137.0 1.0 constant_dynamic-slice_fusion.2
  138.7 1.4 fusion.86
  140.1 2.2 fusion.89
  142.8 1.0 constant_dynamic-slice_fusion.2
  144.4 1.4 fusion.86
  145.9 2.2 fusion.89
  148.5 1.0 constant_dynamic-slice_fusion.2
  150.1 1.4 fusion.86
  151.6 2.2 fusion.89
  154.3 1.0 constant_dynamic-slice_fusion.2
  155.9 1.4 fusion.86
  157.3 2.2 fusion.89
  161.6 1.4 fusion.86
  163.1 2.2 fusion.89
  167.4 1.4 fusion.86
  168.8 2.2 fusion.89
  171.5 9.1 %all_to_all.20 = f32[8,8,128]{2,1,0:T(8,128)S(1)} all-to-all(f32[8,8,128]{2,1,0:T(8,128)S(1)} %get-tuple-element.50), channel_id=1, replica_groups=mesh['span'=8,'tensor'=4] {'span'}, dimensions={0} | all-to-all | bytes 65536 | tf_op jit(solution)/shard_map/all_to_all | solution.py:93
  180.5 9.0 %all_to_all.21 = f32[8,8,128]{2,1,0:T(8,128)S(1)} all-to-all(f32[8,8,128]{2,1,0:T(8,128)S(1)} %get-tuple-element.51), channel_id=1, replica_groups=mesh['span'=8,'tensor'=4] {'span'}, dimensions={0} | all-to-all | bytes 65536 | tf_op jit(solution)/shard_map/all_to_all | solution.py:93
  189.6 4.5 %all-to-all-start = ((f32[8,8,128,128]{3,2,1,0:T(8,128)}), f32[8,8,128,128]{3,2,1,0:T(8,128)}, u32[]{:S(2)}, u32[]{:S(2)}) async-start(f32[8,8,128,128]{3,2,1,0:T(8,128)} %get-tuple-element.49), calls=%async_computation | async-start | bytes 8388608 | tf_op jit(solution)/shard_map/all_to_all | solution.py:93
  194.2 6.2 %convolution_convert_fusion.1 = bf16[128,1024]{1,0:T(8,128)(2,1)} fusion(bf16[128,5120]{1,0:T(8,128)(2,1)S(1)} %copy-done, bf16[5120,1024]{1,0:T(8,128)(2,1)} %param.17), kind=kOutput, calls=%fused_computation.45 | convolution fusion | flops 1342308352 | bytes 12058624 | tf_op jit(solution)/shard_map/dot_general | solution.py:66
  202.1 2.2 copy.43
  204.3 93.9 %all-gather.8.cloned.1.call-done = bf16[1024,1024]{1,0:T(8,128)(2,1)} async-done(((bf16[128,1024]{1,0:T(8,128)(2,1)}), bf16[1024,1024]{1,0:T(8,128)(2,1)}) %all-gather.8.cloned.1.call-update) | async-done | bytes 2097168 | tf_op jit(solution)/shard_map/all_gather | solution.py:107
  298.2 3.9 %copy.37 = bf16[1024,1024]{0,1:T(8,128)(2,1)} copy(bf16[1024,1024]{1,0:T(8,128)(2,1)} %all-gather.8.cloned.1.call-done) | data formatting | bytes 4194304 | tf_op jit(solution)/shard_map/reshape | solution.py:15
  302.2 2.9 fusion.19
  305.1 3.5 fusion.20
  308.6 2.3 all-to-all-done
  310.8 2.9 multiply_reduce_fusion
  313.9 3.6 fusion.40
  317.5 6.6 %convolution_convert_fusion = bf16[128,5120]{1,0:T(8,128)(2,1)} fusion(bf16[128,1024]{0,1:T(8,128)(2,1)S(1)} %bitcast.115, bf16[1024,5120]{1,0:T(8,128)(2,1)} %param.18), kind=kOutput, calls=%fused_computation.28 | convolution fusion | flops 1342832640 | bytes 12058624 | tf_op jit(solution)/shard_map/dot_general | solution.py:122
  324.2 25.2 %reduce-scatter.2.cloned.1.call-done = bf16[32,5120]{1,0:T(8,128)(2,1)} async-done(((bf16[128,5120]{1,0:T(8,128)(2,1)}), bf16[32,5120]{1,0:T(8,128)(2,1)}) %reduce-scatter.2.cloned.1.call-update) | async-done | bytes 327696 | tf_op jit(solution)/shard_map/reduce_scatter | solution.py:121
  349.4 1.8 multiply_convert_fusion
  (70 shorter events, 13.4 us)
Async XLA Ops:
  6.5 27.3 %all-gather.4.cloned.1.call-start = ((), (), s32[]{:S(2)}) async-start(), calls=%async_computation.5 | async-start | bytes 1638400 | tf_op jit(solution)/shard_map/all_gather | solution.py:64
  12.7 109.3 %all-gather.6.cloned.1.call-start = ((), (), s32[]{:S(2)}) async-start(), calls=%async_computation.6 | async-start | bytes 2359296 | tf_op jit(solution)/shard_map/all_gather | solution.py:85
  33.8 6.8 %copy-start = (bf16[128,5120]{1,0:T(8,128)(2,1)S(1)}, bf16[128,5120]{1,0:T(8,128)(2,1)}, u32[]{:S(2)}) copy-start(bf16[128,5120]{1,0:T(8,128)(2,1)} %all-gather.4.cloned.1.call-done) | copy-start | bytes 3932164
  47.7 123.8 %all-to-all-start.2 = ((bf16[8,128,1024]{2,1,0:T(8,128)(2,1)}), bf16[8,128,1024]{2,1,0:T(8,128)(2,1)S(1)}, u32[]{:S(2)}, u32[]{:S(2)}) async-start(bf16[8,128,1024]{2,1,0:T(8,128)(2,1)} %stack.2), calls=%async_computation.2 | async-start | bytes 4194304 | tf_op jit(solution)/shard_map/all_to_all | solution.py:105
  171.5 18.1 %copy-start.1 = (bf16[8,128,1024]{2,1,0:T(8,128)(2,1)}, bf16[8,128,1024]{2,1,0:T(8,128)(2,1)S(1)}, u32[]{:S(2)}) copy-start(bf16[8,128,1024]{2,1,0:T(8,128)(2,1)S(1)} %all-to-all-done.2) | copy-start | bytes 6291460
  189.6 121.3 %all-to-all-start = ((f32[8,8,128,128]{3,2,1,0:T(8,128)}), f32[8,8,128,128]{3,2,1,0:T(8,128)}, u32[]{:S(2)}, u32[]{:S(2)}) async-start(f32[8,8,128,128]{3,2,1,0:T(8,128)} %get-tuple-element.49), calls=%async_computation | async-start | bytes 8388608 | tf_op jit(solution)/shard_map/all_to_all | solution.py:93
  194.1 6.5 %copy-start.4 = (s32[8]{0:T(128)S(1)}, s32[8]{0:T(128)}, u32[]{:S(2)}) copy-start(s32[8]{0:T(128)} %param.22) | copy-start | bytes 100
  194.2 104.1 %all-gather.8.cloned.1.call-start = ((), (), s32[]{:S(2)}) async-start(), calls=%async_computation.7 | async-start | bytes 2359296 | tf_op jit(solution)/shard_map/all_gather | solution.py:107
  200.4 148.9 %reduce-scatter.2.cloned.1.call-start = ((), (), s32[]{:S(2)}) async-start(), calls=%async_computation.8 | async-start | bytes 1638400 | tf_op jit(solution)/shard_map/reduce_scatter | solution.py:121
  202.0 100.1 %copy-start.2 = (bf16[128,1024]{1,0:T(8,128)(2,1)S(1)}, bf16[128,1024]{1,0:T(8,128)(2,1)}, u32[]{:S(2)}) copy-start(bf16[128,1024]{1,0:T(8,128)(2,1)} %convolution_convert_fusion.3) | copy-start | bytes 786436
  305.1 8.8 %copy-start.3 = (bf16[1024,1024]{0,1:T(8,128)(2,1)S(1)}, bf16[1024,1024]{0,1:T(8,128)(2,1)}, u32[]{:S(2)}) copy-start(bf16[1024,1024]{0,1:T(8,128)(2,1)} %copy.37) | copy-start | bytes 6291460
Sparse Core Ops, SparseCore 0:
  12.9 20.8 all-gather.3
  40.6 81.3 all-gather.5
  200.6 97.6 all-gather.7
  324.3 25.0 reduce-scatter.1
